TPU v7x, 32 devices: a whole 2x2x4 slice. The times are simulated.
32 devices in a mesh: dev: 32 (over z, y, x, core).
Axes of the slice: x: 2, y: 2, z: 4, core: 2. Of those that a mesh axis runs over, the one named last changes fastest.
Arguments:
- tensor_tiles: bfloat16 [128, 64, 128, 128], P('dev'), may hold values from -196608 to 196608
- tile_coords: int32 [128, 3], P('dev'), may hold values from 0 to 31, as said below
- tile_count: int32 [32], P('dev'), may hold values from 1 to 4, as said below
- owned_i: int32 [32], P('dev'), may hold values from 0 to 31, as said below
- owned_j: int32 [32], P('dev'), may hold values from 0 to 31, as said below
- owned_k: int32 [32], P('dev'), may hold values from 0 to 31, as said below
- factor_a: float32 [32, 64, 512], P('dev'), may hold values from 0 to 7
- factor_b: float32 [32, 128, 512], P('dev'), may hold values from 0 to 7
- factor_c: float32 [32, 128, 512], P('dev'), may hold values from 0 to 7
- dual_a: float32 [32, 64, 512], P('dev'), may hold values from -1.75 to 1.75
- dual_b: float32 [32, 128, 512], P('dev'), may hold values from -1.75 to 1.75
- dual_c: float32 [32, 128, 512], P('dev'), may hold values from -1.75 to 1.75
- penalty: float32 [3], replicated, may hold values from 0.5 to 2
Outputs:
- factor_a_new: float32 [32, 64, 512], P('dev')
- dual_a_new: float32 [32, 64, 512], P('dev')
- factor_b_new: float32 [32, 128, 512], P('dev')
- dual_b_new: float32 [32, 128, 512], P('dev')
- factor_c_new: float32 [32, 128, 512], P('dev')
- dual_c_new: float32 [32, 128, 512], P('dev')
Inputs may be any that keep to these rules, and one draw needn't show every extreme that they name: `owned_i`: each block number appears once. `owned_j`: each block number appears once. `owned_k`: each block number appears once. `tile_coords`: for a live slot on device d, the block named for each mode is owned by a device d + o with o between -2 and 2, counted around the axis; slots may name the same blocks, and their tiles then add; slots that are not live hold arbitrary block numbers. `tile_count`: some device has all 4 slots live.
All inputs are finite; a program needn't handle non-finite values.
Results may differ from a plain program's by a relative error of at most 0.0025.
The roundings to bfloat16 on the way count: a program that leaves them out, or rounds other values in their place, can miss the bound.
Values may be sent and summed in bfloat16 or wider, within the bound.
A program may use at most 128 MiB of HBM per device.

v0:
```python
import jax
import jax.numpy as jnp
from jax import lax
from jax.sharding import PartitionSpec as P

ITERS = 6
REACH = 2


def for_sending(array):
    return jax.tree.map(lambda a: a.astype(jnp.bfloat16) if a.dtype == jnp.float32 else a, array)


def passed_along(block, axis, distance):
    devices = range(lax.axis_size(axis))
    route = [((i - distance) % len(devices), i) for i in devices]
    return lax.ppermute(block, axis, route)


def chol_solve(chol_low, right_side):
    middle = lax.linalg.triangular_solve(chol_low, right_side, left_side=True, lower=True)
    return lax.linalg.triangular_solve(
        chol_low, middle, left_side=True, lower=True, transpose_a=True
    )


def gram_local(factor):
    flat_rows = factor.reshape(-1, factor.shape[-1])
    return lax.dot_general(
        flat_rows,
        flat_rows,
        (((0,), (0,)), ((), ())),
        precision=lax.Precision.HIGHEST,
        preferred_element_type=jnp.float32,
    )


def window_offsets():
    offsets = [0]
    for distance in range(1, REACH + 1):
        offsets.append(distance)
        offsets.append(-distance)
    return offsets


def neighbour(payload, offset):
    return jax.tree.map(
        lambda part, own: part.astype(own.dtype),
        passed_along(for_sending(payload), "dev", -offset),
        payload,
    )


def expand(payload):
    result = [payload]
    for offset in window_offsets()[1:]:
        result.append(neighbour(payload, offset))
    return result


def fold(totals):
    offsets = window_offsets()
    result = totals[0]
    for place_index in range(1, len(offsets)):
        result = result + passed_along(totals[place_index], "dev", offsets[place_index])
    return result


def position(window_ids, block_id):
    return jnp.sum(
        jnp.where(window_ids == block_id, jnp.arange(window_ids.shape[0], dtype=jnp.int32), 0)
    )


def admm_update(mttkrp, factor, dual_var, gram_mat, weight):
    rank_size = gram_mat.shape[0]
    rho_value = weight * jnp.trace(gram_mat) / rank_size
    identity = jnp.eye(rank_size, dtype=jnp.float32)
    chol_low = jnp.linalg.cholesky(gram_mat + rho_value * identity)
    inverse = chol_solve(chol_low, identity)
    for sweep_index in range(ITERS):
        auxiliary = jnp.dot(
            mttkrp + rho_value * (factor + dual_var),
            inverse,
            precision=lax.Precision.HIGHEST,
            preferred_element_type=jnp.float32,
        )
        factor = jnp.maximum(auxiliary - dual_var, 0.0)
        dual_var = dual_var + factor - auxiliary
    return (factor, dual_var)


def per_device(
    tensor_tiles,
    tile_coords,
    tile_count,
    owned_i,
    owned_j,
    owned_k,
    factor_a,
    factor_b,
    factor_c,
    dual_a,
    dual_b,
    dual_c,
    penalty,
):
    slot_count, rows_first, rows_second, rows_third = tensor_tiles.shape
    rank_size = factor_a.shape[2]
    count_live = tile_count[0]
    win_count = len(window_offsets())
    gram_b, gram_c = lax.psum((gram_local(factor_b), gram_local(factor_c)), "dev")
    own_ids = jnp.concatenate([owned_i, owned_j, owned_k])
    first_window = expand(
        (factor_b[0].astype(jnp.bfloat16), factor_c[0].astype(jnp.bfloat16), own_ids)
    )
    win_b = jnp.stack([member[0] for member in first_window])
    win_c = jnp.stack([member[1] for member in first_window])
    ids_window = jnp.stack([member[2] for member in first_window])

    def slice_tile(slot_index):
        return lax.dynamic_index_in_dim(tensor_tiles, slot_index, 0, keepdims=False)

    def first_part(tile_now, coord_row):
        third_rows = win_c[position(ids_window[:, 2], coord_row[2])]
        flat_tile = tile_now.reshape(rows_first * rows_second, rows_third)
        partial_value = jnp.dot(flat_tile, third_rows, preferred_element_type=jnp.float32)
        return partial_value.reshape(rows_first, rows_second, rank_size)

    def mode_first(slot_index, loop_carry):
        totals = loop_carry[0]
        coord_row = tile_coords[slot_index]
        partial_value = first_part(slice_tile(slot_index), coord_row)
        second_rows = win_b[position(ids_window[:, 1], coord_row[1])]
        contrib = jnp.sum(partial_value * second_rows[None, :, :], axis=1)
        totals = totals.at[position(ids_window[:, 0], coord_row[0])].add(contrib)
        return (totals,)

    start_first = jnp.zeros((win_count, rows_first, rank_size), jnp.float32)
    first_carry = (start_first,)
    first_result = lax.fori_loop(0, count_live, mode_first, first_carry)
    mttkrp_a = fold(first_result[0])
    factor_a_new, dual_a_new = admm_update(
        mttkrp_a, factor_a[0], dual_a[0], gram_b * gram_c, penalty[0]
    )
    gram_a = lax.psum(gram_local(factor_a_new), "dev")
    second_window = expand((factor_a_new.astype(jnp.bfloat16),))
    win_a = jnp.stack([member[0] for member in second_window])

    def mode_second(slot_index, loop_carry):
        totals = loop_carry[0]
        coord_row = tile_coords[slot_index]
        partial_value = first_part(slice_tile(slot_index), coord_row)
        first_rows = win_a[position(ids_window[:, 0], coord_row[0])]
        contrib = jnp.sum(partial_value * first_rows[:, None, :], axis=0)
        totals = totals.at[position(ids_window[:, 1], coord_row[1])].add(contrib)
        return (totals,) + tuple(loop_carry[1:])

    second_carry = (jnp.zeros((win_count, rows_second, rank_size), jnp.float32),) + tuple(
        first_result[1:]
    )
    second_result = lax.fori_loop(0, count_live, mode_second, second_carry)
    mttkrp_b = fold(second_result[0])
    factor_b_new, dual_b_new = admm_update(
        mttkrp_b, factor_b[0], dual_b[0], gram_a * gram_c, penalty[1]
    )
    gram_bn = lax.psum(gram_local(factor_b_new), "dev")
    third_window = expand((factor_b_new.astype(jnp.bfloat16),))
    win_bn = jnp.stack([member[0] for member in third_window])

    def mode_third(slot_index, loop_carry):
        totals = loop_carry[0]
        coord_row = tile_coords[slot_index]
        tile_now = slice_tile(slot_index)
        first_rows = win_a[position(ids_window[:, 0], coord_row[0])]
        flat_tile = tile_now.reshape(rows_first, rows_second * rows_third)
        crossed = lax.dot_general(
            flat_tile, first_rows, (((0,), (0,)), ((), ())), preferred_element_type=jnp.float32
        )
        crossed = crossed.reshape(rows_second, rows_third, rank_size)
        second_rows = win_bn[position(ids_window[:, 1], coord_row[1])]
        contrib = jnp.sum(crossed * second_rows[:, None, :], axis=0)
        totals = totals.at[position(ids_window[:, 2], coord_row[2])].add(contrib)
        return (totals,)

    third_result = lax.fori_loop(
        0, count_live, mode_third, (jnp.zeros((win_count, rows_third, rank_size), jnp.float32),)
    )
    mttkrp_c = fold(third_result[0])
    factor_c_new, dual_c_new = admm_update(
        mttkrp_c, factor_c[0], dual_c[0], gram_a * gram_bn, penalty[2]
    )
    return (
        factor_a_new[None],
        dual_a_new[None],
        factor_b_new[None],
        dual_b_new[None],
        factor_c_new[None],
        dual_c_new[None],
    )


def solution(mesh):
    return jax.shard_map(
        per_device,
        mesh=mesh,
        in_specs=(
            P("dev", None, None, None),
            P("dev", None),
            P("dev"),
            P("dev"),
            P("dev"),
            P("dev"),
            P("dev", None, None),
            P("dev", None, None),
            P("dev", None, None),
            P("dev", None, None),
            P("dev", None, None),
            P("dev", None, None),
            P(),
        ),
        out_specs=(
            P("dev", None, None),
            P("dev", None, None),
            P("dev", None, None),
            P("dev", None, None),
            P("dev", None, None),
            P("dev", None, None),
        ),
        check_vma=False,
    )
```

profile of v0, /device:TPU:0, one launch (start us, length us, event | category | flops | bytes accessed | tf_op | source)
XLA Modules:
  0.0 1002.3 jit_solution(10114383606782808656)
XLA Ops:
  56.0 30.8 %while.45 = (s32[]{:T(128)}, f32[5,64,512]{2,1,0:T(8,128)S(1)}, s32[]{:T(128)}, s32[5,3]{0,1:T(4,128)S(1)}, s32[4,3]{1,0:T(4,128)S(1)}, /*index=5*/bf16[4,64,128...) while((s32[]{:T(128)}, f32[5,64,512]{2,1,0:T(8,128)S(1)}, ...), condition=%wide.region_6.7_spmd, body=%wide.region_0.6_spmd.sunk | while | flops 1082228736 | bytes 3408315 | solution.py:141
  87.7 33.0 %collective-permute-start.12 = (f32[64,512]{1,0:T(8,128)S(1)}, f32[64,512]{1,0:T(8,128)S(1)}, u32[]{:S(2)}, u32[]{:S(2)}) collective-permute-start(f32[64,512]{1,0:T(8,128)S(1)} %get-tuple-element.389), channel_id=1, source_target_pairs={{31,0},{0,1},{1,2},{2,3},{3,4},{4,5},{5,6},{6,7},{7,8},{8,9},{9,10... | collective-permute-start | bytes 393224 | tf_op jit(solution)/shard_map/ppermute | solution.py:17
  131.0 36.6 %all-reduce.10.cloned.1.call-done = (f32[512,512]{0,1:T(8,128)}, f32[512,512]{0,1:T(8,128)}) async-done(((f32[512,512]{0,1:T(8,128)}, f32[512,512]{0,1:T(8,128)}), (f32[512,512]{0,1:T(8,128)}, f32[512,512]{0,1:T(8,128)})) %all-reduce.10.cloned.1.call-update) | async-done | bytes 2097168 | tf_op jit(solution)/shard_map/psum | solution.py:112
  175.1 11.7 %cholesky.374 = f32[128,128]{1,0:T(8,128)S(1)} custom-call(f32[128,128]{1,0:T(8,128)S(1)} %cholesky.586), custom_call_target="Cholesky" | custom-call | tf_op jit(solution)/shard_map/jit(cholesky)/cholesky | solution.py:79
  186.9 9.8 custom-call.36
  199.3 11.7 %cholesky.393 = f32[128,128]{1,0:T(8,128)S(1)} custom-call(f32[128,128]{1,0:T(8,128)S(1)} %cholesky.590), custom_call_target="Cholesky" | custom-call | tf_op jit(solution)/shard_map/jit(cholesky)/cholesky | solution.py:79
  211.1 10.0 custom-call.37
  222.6 11.7 %cholesky.414 = f32[128,128]{1,0:T(8,128)S(1)} custom-call(f32[128,128]{1,0:T(8,128)S(1)} %cholesky.595), custom_call_target="Cholesky" | custom-call | tf_op jit(solution)/shard_map/jit(cholesky)/cholesky | solution.py:79
  235.0 9.8 custom-call.38
  246.3 11.7 %cholesky.431 = f32[128,128]{1,0:T(8,128)S(1)} custom-call(f32[128,128]{1,0:T(8,128)S(1)} %convolution_subtract_fusion.26), custom_call_target="Cholesky" | custom-call | tf_op jit(solution)/shard_map/jit(cholesky)/cholesky | solution.py:79
  270.1 39.7 %custom-call.40 = f32[4,128,128]{1,2,0:T(8,128)S(1)} custom-call(f32[4,128,128]{2,1,0:T(8,128)S(1)} %get-tuple-element.218), custom_call_target="InvertDiagBlocksLowerTriangular" | custom-call | tf_op jit(solution)/shard_map/triangular_solve/custom-call.8 | solution.py:22
  335.7 30.8 %while.46 = (s32[]{:T(128)}, f32[5,128,512]{2,1,0:T(8,128)S(1)}, s32[]{:T(128)}, s32[5,3]{0,1:T(4,128)S(1)}, s32[4,3]{1,0:T(4,128)S(1)}, /*index=5*/bf16[4,64,12...) while((s32[]{:T(128)}, f32[5,128,512]{2,1,0:T(8,128)S(1)}, ...), condition=%wide.region_24.28_spmd, body=%wide.region_18.27_spmd.sunk | while | flops 1082228736 | bytes 3604923 | solution.py:162
  368.2 32.2 %collective-permute-start.20 = (f32[128,512]{1,0:T(8,128)}, f32[128,512]{1,0:T(8,128)}, u32[]{:S(2)}, u32[]{:S(2)}) collective-permute-start(f32[128,512]{1,0:T(8,128)} %get-tuple-element.383), channel_id=1, source_target_pairs={{31,0},{0,1},{1,2},{2,3},{3,4},{4,5},{5,6},{6,7},{7,8},{8,9},{9,10... | collective-permute-start | bytes 786440 | tf_op jit(solution)/shard_map/ppermute | solution.py:17
  418.1 118.1 %all-reduce.6.cloned.1.call-done = f32[512,512]{0,1:T(8,128)} async-done(((f32[512,512]{0,1:T(8,128)}), f32[512,512]{0,1:T(8,128)}) %all-reduce.6.cloned.1.call-update) | async-done | bytes 1048592 | tf_op jit(solution)/shard_map/psum | solution.py:146
  543.4 11.7 %cholesky.446 = f32[128,128]{1,0:T(8,128)S(1)} custom-call(f32[128,128]{1,0:T(8,128)S(1)} %cholesky.599), custom_call_target="Cholesky" | custom-call | tf_op jit(solution)/shard_map/jit(cholesky)/cholesky | solution.py:79
  555.3 9.8 custom-call.41
  567.6 11.7 %cholesky.465 = f32[128,128]{1,0:T(8,128)S(1)} custom-call(f32[128,128]{1,0:T(8,128)S(1)} %cholesky.603), custom_call_target="Cholesky" | custom-call | tf_op jit(solution)/shard_map/jit(cholesky)/cholesky | solution.py:79
  580.7 10.2 %custom-call.42 = f32[1,128,128]{1,2,0:T(8,128)S(1)} custom-call(f32[1,128,128]{2,1,0:T(8,128)S(1)} %get-tuple-element.413), custom_call_target="InvertDiagBlocksLowerTriangular" | custom-call | tf_op jit(solution)/shard_map/jit(cholesky)/cholesky | solution.py:79
  592.4 11.7 %cholesky.486 = f32[128,128]{1,0:T(8,128)S(1)} custom-call(f32[128,128]{1,0:T(8,128)S(1)} %cholesky.608), custom_call_target="Cholesky" | custom-call | tf_op jit(solution)/shard_map/jit(cholesky)/cholesky | solution.py:79
  604.8 9.8 custom-call.43
  616.1 11.9 %cholesky.503 = f32[128,128]{1,0:T(8,128)S(1)} custom-call(f32[128,128]{1,0:T(8,128)S(1)} %convolution_subtract_fusion.25), custom_call_target="Cholesky" | custom-call | tf_op jit(solution)/shard_map/jit(cholesky)/cholesky | solution.py:79
  639.5 39.3 %custom-call.45 = f32[4,128,128]{1,2,0:T(8,128)S(1)} custom-call(f32[4,128,128]{2,1,0:T(8,128)S(1)} %get-tuple-element.220), custom_call_target="InvertDiagBlocksLowerTriangular" | custom-call | tf_op jit(solution)/shard_map/triangular_solve/custom-call.8 | solution.py:22
  704.3 40.4 %while.47 = (s32[]{:T(128)}, f32[5,128,512]{2,1,0:T(8,128)S(1)}, s32[]{:T(128)}, s32[5,3]{0,1:T(4,128)S(1)}, s32[4,3]{1,0:T(4,128)S(1)}, /*index=5*/bf16[4,64,12...) while((s32[]{:T(128)}, f32[5,128,512]{2,1,0:T(8,128)S(1)}, ...), condition=%wide.region_33.37_spmd, body=%wide.region_27.36_spmd.sunk | while | flops 1090650112 | bytes 8061371 | solution.py:186
  744.8 42.1 %collective-permute-start.28 = (f32[128,512]{1,0:T(8,128)S(1)}, f32[128,512]{1,0:T(8,128)S(1)}, u32[]{:S(2)}, u32[]{:S(2)}) collective-permute-start(f32[128,512]{1,0:T(8,128)S(1)} %get-tuple-element.379), channel_id=1, source_target_pairs={{31,0},{0,1},{1,2},{2,3},{3,4},{4,5},{5,6},{6,7},{7,8},{8,9},{9,10... | collective-permute-start | bytes 786440 | tf_op jit(solution)/shard_map/ppermute | solution.py:17
  802.8 36.4 %all-reduce.8.cloned.1.call-done = f32[512,512]{0,1:T(8,128)} async-done(((f32[512,512]{0,1:T(8,128)}), f32[512,512]{0,1:T(8,128)}) %all-reduce.8.cloned.1.call-update) | async-done | bytes 1048592 | tf_op jit(solution)/shard_map/psum | solution.py:167
  846.4 11.7 %cholesky.518 = f32[128,128]{1,0:T(8,128)S(1)} custom-call(f32[128,128]{1,0:T(8,128)S(1)} %cholesky.612), custom_call_target="Cholesky" | custom-call | tf_op jit(solution)/shard_map/jit(cholesky)/cholesky | solution.py:79
  858.3 9.8 custom-call.46
  870.6 11.7 %cholesky.537 = f32[128,128]{1,0:T(8,128)S(1)} custom-call(f32[128,128]{1,0:T(8,128)S(1)} %cholesky.616), custom_call_target="Cholesky" | custom-call | tf_op jit(solution)/shard_map/jit(cholesky)/cholesky | solution.py:79
  883.7 10.0 custom-call.47
  895.2 11.7 %cholesky.558 = f32[128,128]{1,0:T(8,128)S(1)} custom-call(f32[128,128]{1,0:T(8,128)S(1)} %cholesky.621), custom_call_target="Cholesky" | custom-call | tf_op jit(solution)/shard_map/jit(cholesky)/cholesky | solution.py:79
  918.9 11.9 %cholesky.575 = f32[128,128]{1,0:T(8,128)S(1)} custom-call(f32[128,128]{1,0:T(8,128)S(1)} %convolution_subtract_fusion.24), custom_call_target="Cholesky" | custom-call | tf_op jit(solution)/shard_map/jit(cholesky)/cholesky | solution.py:79
  942.8 39.3 %custom-call.50 = f32[4,128,128]{1,2,0:T(8,128)S(1)} custom-call(f32[4,128,128]{2,1,0:T(8,128)S(1)} %get-tuple-element.222), custom_call_target="InvertDiagBlocksLowerTriangular" | custom-call | tf_op jit(solution)/shard_map/triangular_solve/custom-call.8 | solution.py:22
  (385 shorter events, 320.1 us)
Async XLA Ops:
  7.2 160.4 %all-reduce.10.cloned.1.call-start = ((), (), s32[]{:S(2)}) async-start(), calls=%async_computation.2 | async-start | bytes 4194304 | tf_op jit(solution)/shard_map/psum | solution.py:112
  9.2 25.0 %collective-permute-start = (s32[3]{0:T(128)S(1)}, s32[3]{0:T(128)S(1)}, u32[]{:S(2)}, u32[]{:S(2)}) collective-permute-start(s32[3]{0:T(128)S(1)} %pad_add_fusion), channel_id=1, source_target_pairs={{1,0},{2,1},{3,2},{4,3},{5,4},{6,5},{7,6},{8,7},{9,8},{10,9},{11,1... | collective-permute-start | bytes 44 | tf_op jit(solution)/shard_map/ppermute | solution.py:17
  15.6 18.6 %collective-permute-start.1 = (s32[3]{0:T(128)S(1)}, s32[3]{0:T(128)S(1)}, u32[]{:S(2)}, u32[]{:S(2)}) collective-permute-start(s32[3]{0:T(128)S(1)} %pad_add_fusion), channel_id=1, source_target_pairs={{31,0},{0,1},{1,2},{2,3},{3,4},{4,5},{5,6},{6,7},{7,8},{8,9},{9,10... | collective-permute-start | bytes 44 | tf_op jit(solution)/shard_map/ppermute | solution.py:17
  15.6 19.0 %collective-permute-start.2 = (s32[3]{0:T(128)S(1)}, s32[3]{0:T(128)S(1)}, u32[]{:S(2)}, u32[]{:S(2)}) collective-permute-start(s32[3]{0:T(128)S(1)} %pad_add_fusion), channel_id=1, source_target_pairs={{2,0},{3,1},{4,2},{5,3},{6,4},{7,5},{8,6},{9,7},{10,8},{11,9},{12,... | collective-permute-start | bytes 44 | tf_op jit(solution)/shard_map/ppermute | solution.py:17
  16.7 19.6 %collective-permute-start.3 = (s32[3]{0:T(128)S(1)}, s32[3]{0:T(128)S(1)}, u32[]{:S(2)}, u32[]{:S(2)}) collective-permute-start(s32[3]{0:T(128)S(1)} %pad_add_fusion), channel_id=1, source_target_pairs={{30,0},{31,1},{0,2},{1,3},{2,4},{3,5},{4,6},{5,7},{6,8},{7,9},{8,1... | collective-permute-start | bytes 44 | tf_op jit(solution)/shard_map/ppermute | solution.py:17
  18.6 26.1 %collective-permute-start.4 = (bf16[128,512]{1,0:T(8,128)(2,1)S(1)}, bf16[128,512]{1,0:T(8,128)(2,1)S(1)}, u32[]{:S(2)}, u32[]{:S(2)}) collective-permute-start(bf16[128,512]{1,0:T(8,128)(2,1)S(1)} %bitcast_convert_fusion.4), channel_id=1, source_target_pairs={{1,0},{2,1},{3,2},{4,3},{5,4},{6,5},{7,6},{8,7},{9,8},{10,9},{11,1... | collective-permute-start | bytes 393224 | tf_op jit(solution)/shard_map/ppermute | solution.py:17
  33.3 503.0 %all-reduce.6.cloned.1.call-start = ((), (), s32[]{:S(2)}) async-start(), calls=%async_computation | async-start | bytes 2097152 | tf_op jit(solution)/shard_map/psum | solution.py:146
  34.2 11.1 %collective-permute-start.5 = (bf16[128,512]{1,0:T(8,128)(2,1)S(1)}, bf16[128,512]{1,0:T(8,128)(2,1)S(1)}, u32[]{:S(2)}, u32[]{:S(2)}) collective-permute-start(bf16[128,512]{1,0:T(8,128)(2,1)S(1)} %bitcast_convert_fusion.4), channel_id=1, source_target_pairs={{31,0},{0,1},{1,2},{2,3},{3,4},{4,5},{5,6},{6,7},{7,8},{8,9},{9,10... | collective-permute-start | bytes 393224 | tf_op jit(solution)/shard_map/ppermute | solution.py:17
  34.2 11.1 %collective-permute-start.6 = (bf16[128,512]{1,0:T(8,128)(2,1)S(1)}, bf16[128,512]{1,0:T(8,128)(2,1)S(1)}, u32[]{:S(2)}, u32[]{:S(2)}) collective-permute-start(bf16[128,512]{1,0:T(8,128)(2,1)S(1)} %bitcast_convert_fusion.4), channel_id=1, source_target_pairs={{2,0},{3,1},{4,2},{5,3},{6,4},{7,5},{8,6},{9,7},{10,8},{11,9},{12,... | collective-permute-start | bytes 393224 | tf_op jit(solution)/shard_map/ppermute | solution.py:17
  34.6 12.8 %collective-permute-start.7 = (bf16[128,512]{1,0:T(8,128)(2,1)S(1)}, bf16[128,512]{1,0:T(8,128)(2,1)S(1)}, u32[]{:S(2)}, u32[]{:S(2)}) collective-permute-start(bf16[128,512]{1,0:T(8,128)(2,1)S(1)} %bitcast_convert_fusion.4), channel_id=1, source_target_pairs={{30,0},{31,1},{0,2},{1,3},{2,4},{3,5},{4,6},{5,7},{6,8},{7,9},{8,1... | collective-permute-start | bytes 393224 | tf_op jit(solution)/shard_map/ppermute | solution.py:17
  36.3 11.4 %collective-permute-start.8 = (bf16[128,512]{1,0:T(8,128)(2,1)S(1)}, bf16[128,512]{1,0:T(8,128)(2,1)S(1)}, u32[]{:S(2)}, u32[]{:S(2)}) collective-permute-start(bf16[128,512]{1,0:T(8,128)(2,1)S(1)} %bitcast_convert_fusion.3), channel_id=1, source_target_pairs={{1,0},{2,1},{3,2},{4,3},{5,4},{6,5},{7,6},{8,7},{9,8},{10,9},{11,1... | collective-permute-start | bytes 393224 | tf_op jit(solution)/shard_map/ppermute | solution.py:17
  44.7 10.2 %collective-permute-start.9 = (bf16[128,512]{1,0:T(8,128)(2,1)S(1)}, bf16[128,512]{1,0:T(8,128)(2,1)S(1)}, u32[]{:S(2)}, u32[]{:S(2)}) collective-permute-start(bf16[128,512]{1,0:T(8,128)(2,1)S(1)} %bitcast_convert_fusion.3), channel_id=1, source_target_pairs={{31,0},{0,1},{1,2},{2,3},{3,4},{4,5},{5,6},{6,7},{7,8},{8,9},{9,10... | collective-permute-start | bytes 393224 | tf_op jit(solution)/shard_map/ppermute | solution.py:17
  45.3 9.6 collective-permute-start.10
  45.3 10.5 %collective-permute-start.11 = (bf16[128,512]{1,0:T(8,128)(2,1)S(1)}, bf16[128,512]{1,0:T(8,128)(2,1)S(1)}, u32[]{:S(2)}, u32[]{:S(2)}) collective-permute-start(bf16[128,512]{1,0:T(8,128)(2,1)S(1)} %bitcast_convert_fusion.3), channel_id=1, source_target_pairs={{30,0},{31,1},{0,2},{1,3},{2,4},{3,5},{4,6},{5,7},{6,8},{7,9},{8,1... | collective-permute-start | bytes 393224 | tf_op jit(solution)/shard_map/ppermute | solution.py:17
  87.7 39.1 %collective-permute-start.12 = (f32[64,512]{1,0:T(8,128)S(1)}, f32[64,512]{1,0:T(8,128)S(1)}, u32[]{:S(2)}, u32[]{:S(2)}) collective-permute-start(f32[64,512]{1,0:T(8,128)S(1)} %get-tuple-element.389), channel_id=1, source_target_pairs={{31,0},{0,1},{1,2},{2,3},{3,4},{4,5},{5,6},{6,7},{7,8},{8,9},{9,10... | collective-permute-start | bytes 393224 | tf_op jit(solution)/shard_map/ppermute | solution.py:17
  120.7 9.8 collective-permute-start.14
  122.4 8.6 collective-permute-start.15
  325.6 7.3 collective-permute-start.17
  325.7 7.3 collective-permute-start.18
  327.7 7.9 collective-permute-start.19
  368.2 39.9 %collective-permute-start.20 = (f32[128,512]{1,0:T(8,128)}, f32[128,512]{1,0:T(8,128)}, u32[]{:S(2)}, u32[]{:S(2)}) collective-permute-start(f32[128,512]{1,0:T(8,128)} %get-tuple-element.383), channel_id=1, source_target_pairs={{31,0},{0,1},{1,2},{2,3},{3,4},{4,5},{5,6},{6,7},{7,8},{8,9},{9,10... | collective-permute-start | bytes 786440 | tf_op jit(solution)/shard_map/ppermute | solution.py:17
  400.4 7.7 collective-permute-start.21
  400.4 12.7 %collective-permute-start.22 = (f32[128,512]{1,0:T(8,128)}, f32[128,512]{1,0:T(8,128)}, u32[]{:S(2)}, u32[]{:S(2)}) collective-permute-start(f32[128,512]{1,0:T(8,128)} %get-tuple-element.385), channel_id=1, source_target_pairs={{30,0},{31,1},{0,2},{1,3},{2,4},{3,5},{4,6},{5,7},{6,8},{7,9},{8,1... | collective-permute-start | bytes 786440 | tf_op jit(solution)/shard_map/ppermute | solution.py:17
  402.0 14.1 %collective-permute-start.23 = (f32[128,512]{1,0:T(8,128)}, f32[128,512]{1,0:T(8,128)}, u32[]{:S(2)}, u32[]{:S(2)}) collective-permute-start(f32[128,512]{1,0:T(8,128)} %get-tuple-element.384), channel_id=1, source_target_pairs={{2,0},{3,1},{4,2},{5,3},{6,4},{7,5},{8,6},{9,7},{10,8},{11,9},{12,... | collective-permute-start | bytes 786440 | tf_op jit(solution)/shard_map/ppermute | solution.py:17
  408.1 431.1 %all-reduce.8.cloned.1.call-start = ((), (), s32[]{:S(2)}) async-start(), calls=%async_computation.1 | async-start | bytes 2097152 | tf_op jit(solution)/shard_map/psum | solution.py:167
  693.3 8.0 collective-permute-start.25
  693.3 8.0 collective-permute-start.26
  695.2 8.9 collective-permute-start.27
  744.8 49.3 %collective-permute-start.28 = (f32[128,512]{1,0:T(8,128)S(1)}, f32[128,512]{1,0:T(8,128)S(1)}, u32[]{:S(2)}, u32[]{:S(2)}) collective-permute-start(f32[128,512]{1,0:T(8,128)S(1)} %get-tuple-element.379), channel_id=1, source_target_pairs={{31,0},{0,1},{1,2},{2,3},{3,4},{4,5},{5,6},{6,7},{7,8},{8,9},{9,10... | collective-permute-start | bytes 786440 | tf_op jit(solution)/shard_map/ppermute | solution.py:17
  786.9 7.2 collective-permute-start.29
  786.9 12.5 %collective-permute-start.30 = (f32[128,512]{1,0:T(8,128)S(1)}, f32[128,512]{1,0:T(8,128)S(1)}, u32[]{:S(2)}, u32[]{:S(2)}) collective-permute-start(f32[128,512]{1,0:T(8,128)S(1)} %get-tuple-element.381), channel_id=1, source_target_pairs={{30,0},{31,1},{0,2},{1,3},{2,4},{3,5},{4,6},{5,7},{6,8},{7,9},{8,1... | collective-permute-start | bytes 786440 | tf_op jit(solution)/shard_map/ppermute | solution.py:17
  788.6 13.3 %collective-permute-start.31 = (f32[128,512]{1,0:T(8,128)S(1)}, f32[128,512]{1,0:T(8,128)S(1)}, u32[]{:S(2)}, u32[]{:S(2)}) collective-permute-start(f32[128,512]{1,0:T(8,128)S(1)} %get-tuple-element.380), channel_id=1, source_target_pairs={{2,0},{3,1},{4,2},{5,3},{6,4},{7,5},{8,6},{9,7},{10,8},{11,9},{12,... | collective-permute-start | bytes 786440 | tf_op jit(solution)/shard_map/ppermute | solution.py:17
  (33 other events, 884.0 us)
Sparse Core Ops, SparseCore 0:
  33.4 134.1 all-reduce.9
  408.2 128.0 all-reduce.5
  697.8 141.2 all-reduce.7
where the time goes:
time: 1010 us; the launch traced here: 1000 us
  other arithmetic  397 us (39%)
  waiting for transfers between devices  234 us (23%)
  starting transfers between devices  162 us (16%)
  matrix products  95.6 us (9%)
  local copies, waits for them, and re-layouts  43.2 us (4%)
  loops' own time  41 us (4%)
  between operations  29 us (3%)
    another operation x44, other arithmetic, admm_update(): chol_low = jnp.linalg.cholesky(gram_mat + rho_value * identity)  238 us
    ppermute x32, starting transfers between devices, passed_along(): return lax.ppermute(block, axis, route)  162 us
    another operation x7, other arithmetic, chol_solve(): lax.linalg.triangular_solve(chol_low, middle, left_side=True, lower=True,...  119 us
    psum x1, waiting for transfers between devices, per_device(): gram_a = lax.psum(gram_local(factor_a_new), 'dev')  118 us
    ppermute x32, waiting for transfers between devices, passed_along(): return lax.ppermute(block, axis, route)  43 us
    psum x1, waiting for transfers between devices, per_device(): lax.psum((gram_local(factor_b), gram_local(factor_c)), 'dev')  36.6 us
    psum x1, waiting for transfers between devices, per_device(): gram_bn = lax.psum(gram_local(factor_b_new), 'dev')  36.4 us
    another operation x40, local copies, waits for them, and re-layouts, chol_solve(): lax.linalg.triangular_solve(chol_low, middle, left_side=True, lower=True,...  24.3 us
  transfers between devices with their start and end apart: 35, of which 17 were waited for; matrix products, arithmetic and copies ran while one was open for 6% of the time, Pallas kernels for 0%

commit v1 on v0

--- a/solution.py
+++ b/solution.py
@@ -143,7 +143,7 @@
     factor_a_new, dual_a_new = admm_update(
         mttkrp_a, factor_a[0], dual_a[0], gram_b * gram_c, penalty[0]
     )
-    gram_a = lax.psum(gram_local(factor_a_new), "dev")
+    gram_a = jnp.sum(lax.all_gather(gram_local(factor_a_new), "dev"), axis=0)
     second_window = expand((factor_a_new.astype(jnp.bfloat16),))
     win_a = jnp.stack([member[0] for member in second_window])
 

time: 1010 us -> 1040 us (1.030)
  other arithmetic: 397 us -> 425 us
  waiting for transfers between devices: 234 us -> 212 us
  local copies, waits for them, and re-layouts: 43.2 us -> 60.2 us
    psum x1 -> x0, waiting for transfers between devices: 118 us -> none  [per_device(): gram_a = lax.psum(gram_local(factor_a_new), 'dev')]
    all_gather x0 -> x1, waiting for transfers between devices: none -> 110 us  [per_device(): gram_a = jnp.sum(lax.all_gather(gram_local(factor_a_new), 'dev'), axis=0)]
    psum x1, waiting for transfers between devices: 36.4 us -> 21.3 us  [per_device(): gram_bn = lax.psum(gram_local(factor_b_new), 'dev')]
    reduce_sum x0 -> x1, other arithmetic: none -> 12.3 us  [per_device(): gram_a = jnp.sum(lax.all_gather(gram_local(factor_a_new), 'dev'), axis=0)]
  transfers between devices with their start and end apart: 35 -> 35, of which waited for: 17 -> 17; matrix products, arithmetic and copies ran while one was open for 6% -> 9% of each run, Pallas kernels for 0% -> 0%
where the time goes in v1:
time: 1040 us; the launch traced here: 1030 us
  other arithmetic  425 us (41%)
  waiting for transfers between devices  212 us (20%)
  starting transfers between devices  169 us (16%)
  matrix products  96.5 us (9%)
  local copies, waits for them, and re-layouts  60.2 us (6%)
  loops' own time  40.1 us (4%)
  between operations  28.9 us (3%)
    another operation x44, other arithmetic, admm_update(): chol_low = jnp.linalg.cholesky(gram_mat + rho_value * identity)  244 us
    ppermute x32, starting transfers between devices, passed_along(): return lax.ppermute(block, axis, route)  169 us
    another operation x7, other arithmetic, chol_solve(): lax.linalg.triangular_solve(chol_low, middle, left_side=True, lower=True,...  121 us
    all_gather x1, waiting for transfers between devices, per_device(): gram_a = jnp.sum(lax.all_gather(gram_local(factor_a_new), 'dev'), axis=0)  110 us
    ppermute x32, waiting for transfers between devices, passed_along(): return lax.ppermute(block, axis, route)  49.3 us
    psum x1, waiting for transfers between devices, per_device(): lax.psum((gram_local(factor_b), gram_local(factor_c)), 'dev')  31.4 us
    another operation x40, local copies, waits for them, and re-layouts, chol_solve(): lax.linalg.triangular_solve(chol_low, middle, left_side=True, lower=True,...  31.1 us
    psum x1, waiting for transfers between devices, per_device(): gram_bn = lax.psum(gram_local(factor_b_new), 'dev')  21.3 us
  transfers between devices with their start and end apart: 35, of which 17 were waited for; matrix products, arithmetic and copies ran while one was open for 9% of the time, Pallas kernels for 0%

profile of v1, /device:TPU:0, one launch (start us, length us, event | category | flops | bytes accessed | tf_op | source)
XLA Modules:
  0.0 1031.4 jit_solution(15153921139527722520)
XLA Ops:
  56.0 31.6 %while.45 = (s32[]{:T(128)}, f32[5,64,512]{2,1,0:T(8,128)S(1)}, s32[]{:T(128)}, s32[5,3]{0,1:T(4,128)S(1)}, s32[4,3]{1,0:T(4,128)}, /*index=5*/bf16[4,64,128,128...) while((s32[]{:T(128)}, f32[5,64,512]{2,1,0:T(8,128)S(1)}, ...), condition=%wide.region_6.7_spmd, body=%wide.region_0.6_spmd.sunk | while | flops 1082228736 | bytes 3408323 | solution.py:141
  88.5 15.9 %collective-permute-start.15 = (f32[64,512]{1,0:T(8,128)S(1)}, f32[64,512]{1,0:T(8,128)S(1)}, u32[]{:S(2)}, u32[]{:S(2)}) collective-permute-start(f32[64,512]{1,0:T(8,128)S(1)} %get-tuple-element.414), channel_id=1, source_target_pairs={{2,0},{3,1},{4,2},{5,3},{6,4},{7,5},{8,6},{9,7},{10,8},{11,9},{12,... | collective-permute-start | bytes 393224 | tf_op jit(solution)/shard_map/ppermute | solution.py:17
  104.5 23.0 %collective-permute-start.13 = (f32[64,512]{1,0:T(8,128)S(1)}, f32[64,512]{1,0:T(8,128)S(1)}, u32[]{:S(2)}, u32[]{:S(2)}) collective-permute-start(f32[64,512]{1,0:T(8,128)S(1)} %get-tuple-element.416), channel_id=1, source_target_pairs={{1,0},{2,1},{3,2},{4,3},{5,4},{6,5},{7,6},{8,7},{9,8},{10,9},{11,1... | collective-permute-start | bytes 393224 | tf_op jit(solution)/shard_map/ppermute | solution.py:17
  137.0 31.4 %all-reduce.7.cloned.1.call-done = (f32[512,512]{0,1:T(8,128)}, f32[512,512]{0,1:T(8,128)}) async-done(((f32[512,512]{0,1:T(8,128)}, f32[512,512]{0,1:T(8,128)}), (f32[512,512]{0,1:T(8,128)}, f32[512,512]{0,1:T(8,128)})) %all-reduce.7.cloned.1.call-update) | async-done | bytes 2097168 | tf_op jit(solution)/shard_map/psum | solution.py:112
  175.9 11.7 %cholesky.374 = f32[128,128]{1,0:T(8,128)S(1)} custom-call(f32[128,128]{1,0:T(8,128)S(1)} %cholesky.586), custom_call_target="Cholesky" | custom-call | tf_op jit(solution)/shard_map/jit(cholesky)/cholesky | solution.py:79
  200.1 11.7 %cholesky.393 = f32[128,128]{1,0:T(8,128)S(1)} custom-call(f32[128,128]{1,0:T(8,128)S(1)} %cholesky.590), custom_call_target="Cholesky" | custom-call | tf_op jit(solution)/shard_map/jit(cholesky)/cholesky | solution.py:79
  223.4 11.7 %cholesky.414 = f32[128,128]{1,0:T(8,128)S(1)} custom-call(f32[128,128]{1,0:T(8,128)S(1)} %cholesky.595), custom_call_target="Cholesky" | custom-call | tf_op jit(solution)/shard_map/jit(cholesky)/cholesky | solution.py:79
  246.4 11.7 %cholesky.431 = f32[128,128]{1,0:T(8,128)S(1)} custom-call(f32[128,128]{1,0:T(8,128)S(1)} %convolution_subtract_fusion.26), custom_call_target="Cholesky" | custom-call | tf_op jit(solution)/shard_map/jit(cholesky)/cholesky | solution.py:79
  270.9 39.7 %custom-call.40 = f32[4,128,128]{1,2,0:T(8,128)S(1)} custom-call(f32[4,128,128]{2,1,0:T(8,128)S(1)} %get-tuple-element.218), custom_call_target="InvertDiagBlocksLowerTriangular" | custom-call | tf_op jit(solution)/shard_map/triangular_solve/custom-call.8 | solution.py:22
  338.4 33.6 %while.46 = (s32[]{:T(128)}, f32[5,128,512]{2,1,0:T(8,128)S(1)}, s32[]{:T(128)}, s32[5,3]{0,1:T(4,128)S(1)}, s32[4,3]{1,0:T(4,128)}, /*index=5*/bf16[4,64,128,12...) while((s32[]{:T(128)}, f32[5,128,512]{2,1,0:T(8,128)S(1)}, ...), condition=%wide.region_24.28_spmd, body=%wide.region_18.27_spmd.sunk | while | flops 1082228736 | bytes 3604931 | solution.py:162
  372.9 16.6 %collective-permute-start.23 = (f32[128,512]{1,0:T(8,128)}, f32[128,512]{1,0:T(8,128)S(1)}, u32[]{:S(2)}, u32[]{:S(2)}) collective-permute-start(f32[128,512]{1,0:T(8,128)} %get-tuple-element.408), channel_id=1, source_target_pairs={{2,0},{3,1},{4,2},{5,3},{6,4},{7,5},{8,6},{9,7},{10,8},{11,9},{12,... | collective-permute-start | bytes 786440 | tf_op jit(solution)/shard_map/ppermute | solution.py:17
  389.5 22.8 %collective-permute-start.21 = (f32[128,512]{1,0:T(8,128)}, f32[128,512]{1,0:T(8,128)S(1)}, u32[]{:S(2)}, u32[]{:S(2)}) collective-permute-start(f32[128,512]{1,0:T(8,128)} %get-tuple-element.410), channel_id=1, source_target_pairs={{1,0},{2,1},{3,2},{4,3},{5,4},{6,5},{7,6},{8,7},{9,8},{10,9},{11,1... | collective-permute-start | bytes 786440 | tf_op jit(solution)/shard_map/ppermute | solution.py:17
  412.4 10.8 %collective-permute-done.21 = f32[128,512]{1,0:T(8,128)S(1)} collective-permute-done((f32[128,512]{1,0:T(8,128)}, f32[128,512]{1,0:T(8,128)S(1)}, u32[]{:S(2)}, u32[]{:S(2)}) %collective-permute-start.21) | collective-permute-done | bytes 262176 | tf_op jit(solution)/shard_map/ppermute | solution.py:17
  428.4 110.0 %all-gather.3.cloned.1.call-done = f32[16384,512]{1,0:T(8,128)} async-done(((f32[512,512]{1,0:T(8,128)}), f32[16384,512]{1,0:T(8,128)}) %all-gather.3.cloned.1.call-update) | async-done | bytes 33554448 | tf_op jit(solution)/shard_map/all_gather | solution.py:146
  538.4 12.3 %reduce_sum.140 = f32[512,512]{1,0:T(8,128)S(1)} reduce(f32[32,512,512]{2,1,0:T(8,128)} %bitcast.569, f32[]{:T(128)} %constant.235.clone.1), dimensions={0}, to_apply=%region_25.29 | reduce | flops 8126464 | bytes 34603012 | tf_op jit(solution)/shard_map/reduce_sum | solution.py:146
  560.4 11.7 %cholesky.446 = f32[128,128]{1,0:T(8,128)S(1)} custom-call(f32[128,128]{1,0:T(8,128)S(1)} %cholesky.599), custom_call_target="Cholesky" | custom-call | tf_op jit(solution)/shard_map/jit(cholesky)/cholesky | solution.py:79
  585.3 11.7 %cholesky.465 = f32[128,128]{1,0:T(8,128)S(1)} custom-call(f32[128,128]{1,0:T(8,128)S(1)} %cholesky.603), custom_call_target="Cholesky" | custom-call | tf_op jit(solution)/shard_map/jit(cholesky)/cholesky | solution.py:79
  597.6 10.2 custom-call.42
  610.9 13.2 %cholesky.486 = f32[128,128]{1,0:T(8,128)} custom-call(f32[128,128]{1,0:T(8,128)} %cholesky.608), custom_call_target="Cholesky" | custom-call | tf_op jit(solution)/shard_map/jit(cholesky)/cholesky | solution.py:79
  626.1 11.3 %custom-call.43 = f32[1,128,128]{1,2,0:T(8,128)} custom-call(f32[1,128,128]{2,1,0:T(8,128)} %get-tuple-element.434), custom_call_target="InvertDiagBlocksLowerTriangular" | custom-call | tf_op jit(solution)/shard_map/jit(cholesky)/cholesky | solution.py:79
  639.7 11.9 %cholesky.503 = f32[128,128]{1,0:T(8,128)S(1)} custom-call(f32[128,128]{1,0:T(8,128)S(1)} %convolution_subtract_fusion.25), custom_call_target="Cholesky" | custom-call | tf_op jit(solution)/shard_map/jit(cholesky)/cholesky | solution.py:79
  659.9 14.0 %while.49 = (s32[]{:T(128)}, f32[512,512]{1,0:T(8,128)}, s32[4,2]{0,1:T(2,128)S(1)}, f32[4,128,128]{2,1,0:T(8,128)}, s32[]{:T(128)}) while((s32[]{:T(128)}, f32[512,512]{1,0:T(8,128)}, s32[4,2]{0,1:T(2,128)S(1)}, f32[4,128,128]{2,1,0:T(8,128)}, s32[]{:T(128)}) %tuple.226), condition=%wide.while_cond.4.clone, body=%wide.while_body.4.clone.sunk | while | flops 2 | bytes 132205 | solution.py:22
  673.9 40.8 %custom-call.45 = f32[4,128,128]{1,2,0:T(8,128)} custom-call(f32[4,128,128]{2,1,0:T(8,128)} %get-tuple-element.220), custom_call_target="InvertDiagBlocksLowerTriangular" | custom-call | tf_op jit(solution)/shard_map/triangular_solve/custom-call.8 | solution.py:22
  744.0 45.0 %while.47 = (s32[]{:T(128)}, f32[5,128,512]{2,1,0:T(8,128)S(1)}, s32[]{:T(128)}, s32[5,3]{0,1:T(4,128)S(1)}, s32[4,3]{1,0:T(4,128)}, /*index=5*/bf16[4,64,128,12...) while((s32[]{:T(128)}, f32[5,128,512]{2,1,0:T(8,128)S(1)}, ...), condition=%wide.region_33.37_spmd, body=%wide.region_27.36_spmd.sunk | while | flops 1090650112 | bytes 9109983 | solution.py:186
  789.2 24.7 %collective-permute-start.31 = (f32[128,512]{1,0:T(8,128)S(1)}, f32[128,512]{1,0:T(8,128)S(1)}, u32[]{:S(2)}, u32[]{:S(2)}) collective-permute-start(f32[128,512]{1,0:T(8,128)S(1)} %get-tuple-element.404), channel_id=1, source_target_pairs={{2,0},{3,1},{4,2},{5,3},{6,4},{7,5},{8,6},{9,7},{10,8},{11,9},{12,... | collective-permute-start | bytes 786440 | tf_op jit(solution)/shard_map/ppermute | solution.py:17
  813.9 27.6 %collective-permute-start.29 = (f32[128,512]{1,0:T(8,128)S(1)}, f32[128,512]{1,0:T(8,128)S(1)}, u32[]{:S(2)}, u32[]{:S(2)}) collective-permute-start(f32[128,512]{1,0:T(8,128)S(1)} %get-tuple-element.406), channel_id=1, source_target_pairs={{1,0},{2,1},{3,2},{4,3},{5,4},{6,5},{7,6},{8,7},{9,8},{10,9},{11,1... | collective-permute-start | bytes 786440 | tf_op jit(solution)/shard_map/ppermute | solution.py:17
  851.7 21.3 %all-reduce.5.cloned.1.call-done = f32[512,512]{0,1:T(8,128)} async-done(((f32[512,512]{0,1:T(8,128)}), f32[512,512]{0,1:T(8,128)}) %all-reduce.5.cloned.1.call-update) | async-done | bytes 1048592 | tf_op jit(solution)/shard_map/psum | solution.py:167
  879.2 11.7 %cholesky.518 = f32[128,128]{1,0:T(8,128)S(1)} custom-call(f32[128,128]{1,0:T(8,128)S(1)} %cholesky.612), custom_call_target="Cholesky" | custom-call | tf_op jit(solution)/shard_map/jit(cholesky)/cholesky | solution.py:79
  901.5 11.7 %cholesky.537 = f32[128,128]{1,0:T(8,128)S(1)} custom-call(f32[128,128]{1,0:T(8,128)S(1)} %cholesky.616), custom_call_target="Cholesky" | custom-call | tf_op jit(solution)/shard_map/jit(cholesky)/cholesky | solution.py:79
  923.9 11.7 %cholesky.558 = f32[128,128]{1,0:T(8,128)S(1)} custom-call(f32[128,128]{1,0:T(8,128)S(1)} %cholesky.621), custom_call_target="Cholesky" | custom-call | tf_op jit(solution)/shard_map/jit(cholesky)/cholesky | solution.py:79
  946.1 11.9 %cholesky.575 = f32[128,128]{1,0:T(8,128)S(1)} custom-call(f32[128,128]{1,0:T(8,128)S(1)} %convolution_subtract_fusion.24), custom_call_target="Cholesky" | custom-call | tf_op jit(solution)/shard_map/jit(cholesky)/cholesky | solution.py:79
  971.8 39.3 %custom-call.50 = f32[4,128,128]{1,2,0:T(8,128)S(1)} custom-call(f32[4,128,128]{2,1,0:T(8,128)S(1)} %get-tuple-element.222), custom_call_target="InvertDiagBlocksLowerTriangular" | custom-call | tf_op jit(solution)/shard_map/triangular_solve/custom-call.8 | solution.py:22
  (383 shorter events, 379.0 us)
Async XLA Ops:
  7.2 161.2 %all-reduce.7.cloned.1.call-start = ((), (), s32[]{:S(2)}) async-start(), calls=%async_computation.2 | async-start | bytes 4194304 | tf_op jit(solution)/shard_map/psum | solution.py:112
  9.2 25.0 %collective-permute-start = (s32[3]{0:T(128)S(1)}, s32[3]{0:T(128)S(1)}, u32[]{:S(2)}, u32[]{:S(2)}) collective-permute-start(s32[3]{0:T(128)S(1)} %pad_add_fusion), channel_id=1, source_target_pairs={{1,0},{2,1},{3,2},{4,3},{5,4},{6,5},{7,6},{8,7},{9,8},{10,9},{11,1... | collective-permute-start | bytes 44 | tf_op jit(solution)/shard_map/ppermute | solution.py:17
  15.6 18.6 %collective-permute-start.1 = (s32[3]{0:T(128)S(1)}, s32[3]{0:T(128)S(1)}, u32[]{:S(2)}, u32[]{:S(2)}) collective-permute-start(s32[3]{0:T(128)S(1)} %pad_add_fusion), channel_id=1, source_target_pairs={{31,0},{0,1},{1,2},{2,3},{3,4},{4,5},{5,6},{6,7},{7,8},{8,9},{9,10... | collective-permute-start | bytes 44 | tf_op jit(solution)/shard_map/ppermute | solution.py:17
  15.6 19.0 %collective-permute-start.2 = (s32[3]{0:T(128)S(1)}, s32[3]{0:T(128)S(1)}, u32[]{:S(2)}, u32[]{:S(2)}) collective-permute-start(s32[3]{0:T(128)S(1)} %pad_add_fusion), channel_id=1, source_target_pairs={{2,0},{3,1},{4,2},{5,3},{6,4},{7,5},{8,6},{9,7},{10,8},{11,9},{12,... | collective-permute-start | bytes 44 | tf_op jit(solution)/shard_map/ppermute | solution.py:17
  16.7 19.6 %collective-permute-start.3 = (s32[3]{0:T(128)S(1)}, s32[3]{0:T(128)S(1)}, u32[]{:S(2)}, u32[]{:S(2)}) collective-permute-start(s32[3]{0:T(128)S(1)} %pad_add_fusion), channel_id=1, source_target_pairs={{30,0},{31,1},{0,2},{1,3},{2,4},{3,5},{4,6},{5,7},{6,8},{7,9},{8,1... | collective-permute-start | bytes 44 | tf_op jit(solution)/shard_map/ppermute | solution.py:17
  18.6 26.1 %collective-permute-start.4 = (bf16[128,512]{1,0:T(8,128)(2,1)S(1)}, bf16[128,512]{1,0:T(8,128)(2,1)S(1)}, u32[]{:S(2)}, u32[]{:S(2)}) collective-permute-start(bf16[128,512]{1,0:T(8,128)(2,1)S(1)} %bitcast_convert_fusion.4), channel_id=1, source_target_pairs={{1,0},{2,1},{3,2},{4,3},{5,4},{6,5},{7,6},{8,7},{9,8},{10,9},{11,1... | collective-permute-start | bytes 393224 | tf_op jit(solution)/shard_map/ppermute | solution.py:17
  33.3 505.1 %all-gather.3.cloned.1.call-start = ((), (), s32[]{:S(2)}) async-start(), calls=%async_computation.1 | async-start | bytes 34603008 | tf_op jit(solution)/shard_map/all_gather | solution.py:146
  34.2 11.1 %collective-permute-start.5 = (bf16[128,512]{1,0:T(8,128)(2,1)S(1)}, bf16[128,512]{1,0:T(8,128)(2,1)S(1)}, u32[]{:S(2)}, u32[]{:S(2)}) collective-permute-start(bf16[128,512]{1,0:T(8,128)(2,1)S(1)} %bitcast_convert_fusion.4), channel_id=1, source_target_pairs={{31,0},{0,1},{1,2},{2,3},{3,4},{4,5},{5,6},{6,7},{7,8},{8,9},{9,10... | collective-permute-start | bytes 393224 | tf_op jit(solution)/shard_map/ppermute | solution.py:17
  34.3 11.2 %collective-permute-start.6 = (bf16[128,512]{1,0:T(8,128)(2,1)S(1)}, bf16[128,512]{1,0:T(8,128)(2,1)S(1)}, u32[]{:S(2)}, u32[]{:S(2)}) collective-permute-start(bf16[128,512]{1,0:T(8,128)(2,1)S(1)} %bitcast_convert_fusion.4), channel_id=1, source_target_pairs={{2,0},{3,1},{4,2},{5,3},{6,4},{7,5},{8,6},{9,7},{10,8},{11,9},{12,... | collective-permute-start | bytes 393224 | tf_op jit(solution)/shard_map/ppermute | solution.py:17
  34.7 12.8 %collective-permute-start.7 = (bf16[128,512]{1,0:T(8,128)(2,1)S(1)}, bf16[128,512]{1,0:T(8,128)(2,1)S(1)}, u32[]{:S(2)}, u32[]{:S(2)}) collective-permute-start(bf16[128,512]{1,0:T(8,128)(2,1)S(1)} %bitcast_convert_fusion.4), channel_id=1, source_target_pairs={{30,0},{31,1},{0,2},{1,3},{2,4},{3,5},{4,6},{5,7},{6,8},{7,9},{8,1... | collective-permute-start | bytes 393224 | tf_op jit(solution)/shard_map/ppermute | solution.py:17
  36.3 11.4 %collective-permute-start.8 = (bf16[128,512]{1,0:T(8,128)(2,1)S(1)}, bf16[128,512]{1,0:T(8,128)(2,1)S(1)}, u32[]{:S(2)}, u32[]{:S(2)}) collective-permute-start(bf16[128,512]{1,0:T(8,128)(2,1)S(1)} %bitcast_convert_fusion.3), channel_id=1, source_target_pairs={{1,0},{2,1},{3,2},{4,3},{5,4},{6,5},{7,6},{8,7},{9,8},{10,9},{11,1... | collective-permute-start | bytes 393224 | tf_op jit(solution)/shard_map/ppermute | solution.py:17
  44.8 10.2 collective-permute-start.9
  45.4 9.6 collective-permute-start.10
  45.4 10.5 %collective-permute-start.11 = (bf16[128,512]{1,0:T(8,128)(2,1)S(1)}, bf16[128,512]{1,0:T(8,128)(2,1)S(1)}, u32[]{:S(2)}, u32[]{:S(2)}) collective-permute-start(bf16[128,512]{1,0:T(8,128)(2,1)S(1)} %bitcast_convert_fusion.3), channel_id=1, source_target_pairs={{30,0},{31,1},{0,2},{1,3},{2,4},{3,5},{4,6},{5,7},{6,8},{7,9},{8,1... | collective-permute-start | bytes 393224 | tf_op jit(solution)/shard_map/ppermute | solution.py:17
  88.5 39.5 %collective-permute-start.15 = (f32[64,512]{1,0:T(8,128)S(1)}, f32[64,512]{1,0:T(8,128)S(1)}, u32[]{:S(2)}, u32[]{:S(2)}) collective-permute-start(f32[64,512]{1,0:T(8,128)S(1)} %get-tuple-element.414), channel_id=1, source_target_pairs={{2,0},{3,1},{4,2},{5,3},{6,4},{7,5},{8,6},{9,7},{10,8},{11,9},{12,... | collective-permute-start | bytes 393224 | tf_op jit(solution)/shard_map/ppermute | solution.py:17
  104.4 23.6 %collective-permute-start.14 = (f32[64,512]{1,0:T(8,128)S(1)}, f32[64,512]{1,0:T(8,128)S(1)}, u32[]{:S(2)}, u32[]{:S(2)}) collective-permute-start(f32[64,512]{1,0:T(8,128)S(1)} %get-tuple-element.415), channel_id=1, source_target_pairs={{30,0},{31,1},{0,2},{1,3},{2,4},{3,5},{4,6},{5,7},{6,8},{7,9},{8,1... | collective-permute-start | bytes 393224 | tf_op jit(solution)/shard_map/ppermute | solution.py:17
  104.5 25.8 %collective-permute-start.13 = (f32[64,512]{1,0:T(8,128)S(1)}, f32[64,512]{1,0:T(8,128)S(1)}, u32[]{:S(2)}, u32[]{:S(2)}) collective-permute-start(f32[64,512]{1,0:T(8,128)S(1)} %get-tuple-element.416), channel_id=1, source_target_pairs={{1,0},{2,1},{3,2},{4,3},{5,4},{6,5},{7,6},{8,7},{9,8},{10,9},{11,1... | collective-permute-start | bytes 393224 | tf_op jit(solution)/shard_map/ppermute | solution.py:17
  127.4 8.9 collective-permute-start.12
  326.0 547.0 %all-reduce.5.cloned.1.call-start = ((), (), s32[]{:S(2)}) async-start(), calls=%async_computation | async-start | bytes 2097152 | tf_op jit(solution)/shard_map/psum | solution.py:167
  327.6 7.9 collective-permute-start.18
  329.6 8.0 collective-permute-start.19
  372.9 39.4 %collective-permute-start.23 = (f32[128,512]{1,0:T(8,128)}, f32[128,512]{1,0:T(8,128)S(1)}, u32[]{:S(2)}, u32[]{:S(2)}) collective-permute-start(f32[128,512]{1,0:T(8,128)} %get-tuple-element.408), channel_id=1, source_target_pairs={{2,0},{3,1},{4,2},{5,3},{6,4},{7,5},{8,6},{9,7},{10,8},{11,9},{12,... | collective-permute-start | bytes 786440 | tf_op jit(solution)/shard_map/ppermute | solution.py:17
  389.5 22.9 %collective-permute-start.22 = (f32[128,512]{1,0:T(8,128)}, f32[128,512]{1,0:T(8,128)S(1)}, u32[]{:S(2)}, u32[]{:S(2)}) collective-permute-start(f32[128,512]{1,0:T(8,128)} %get-tuple-element.409), channel_id=1, source_target_pairs={{30,0},{31,1},{0,2},{1,3},{2,4},{3,5},{4,6},{5,7},{6,8},{7,9},{8,1... | collective-permute-start | bytes 786440 | tf_op jit(solution)/shard_map/ppermute | solution.py:17
  389.5 33.6 %collective-permute-start.21 = (f32[128,512]{1,0:T(8,128)}, f32[128,512]{1,0:T(8,128)S(1)}, u32[]{:S(2)}, u32[]{:S(2)}) collective-permute-start(f32[128,512]{1,0:T(8,128)} %get-tuple-element.410), channel_id=1, source_target_pairs={{1,0},{2,1},{3,2},{4,3},{5,4},{6,5},{7,6},{8,7},{9,8},{10,9},{11,1... | collective-permute-start | bytes 786440 | tf_op jit(solution)/shard_map/ppermute | solution.py:17
  412.4 14.3 %collective-permute-start.20 = (f32[128,512]{1,0:T(8,128)}, f32[128,512]{1,0:T(8,128)}, u32[]{:S(2)}, u32[]{:S(2)}) collective-permute-start(f32[128,512]{1,0:T(8,128)} %get-tuple-element.407), channel_id=1, source_target_pairs={{31,0},{0,1},{1,2},{2,3},{3,4},{4,5},{5,6},{6,7},{7,8},{8,9},{9,10... | collective-permute-start | bytes 786440 | tf_op jit(solution)/shard_map/ppermute | solution.py:17
  732.8 8.0 collective-permute-start.25
  732.8 8.6 collective-permute-start.26
  734.3 8.9 collective-permute-start.27
  789.2 53.9 %collective-permute-start.31 = (f32[128,512]{1,0:T(8,128)S(1)}, f32[128,512]{1,0:T(8,128)S(1)}, u32[]{:S(2)}, u32[]{:S(2)}) collective-permute-start(f32[128,512]{1,0:T(8,128)S(1)} %get-tuple-element.404), channel_id=1, source_target_pairs={{2,0},{3,1},{4,2},{5,3},{6,4},{7,5},{8,6},{9,7},{10,8},{11,9},{12,... | collective-permute-start | bytes 786440 | tf_op jit(solution)/shard_map/ppermute | solution.py:17
  813.9 29.2 %collective-permute-start.30 = (f32[128,512]{1,0:T(8,128)S(1)}, f32[128,512]{1,0:T(8,128)S(1)}, u32[]{:S(2)}, u32[]{:S(2)}) collective-permute-start(f32[128,512]{1,0:T(8,128)S(1)} %get-tuple-element.405), channel_id=1, source_target_pairs={{30,0},{31,1},{0,2},{1,3},{2,4},{3,5},{4,6},{5,7},{6,8},{7,9},{8,1... | collective-permute-start | bytes 786440 | tf_op jit(solution)/shard_map/ppermute | solution.py:17
  813.9 31.5 %collective-permute-start.29 = (f32[128,512]{1,0:T(8,128)S(1)}, f32[128,512]{1,0:T(8,128)S(1)}, u32[]{:S(2)}, u32[]{:S(2)}) collective-permute-start(f32[128,512]{1,0:T(8,128)S(1)} %get-tuple-element.406), channel_id=1, source_target_pairs={{1,0},{2,1},{3,2},{4,3},{5,4},{6,5},{7,6},{8,7},{9,8},{10,9},{11,1... | collective-permute-start | bytes 786440 | tf_op jit(solution)/shard_map/ppermute | solution.py:17
  841.4 9.4 collective-permute-start.28
  (31 other events, 376.9 us)
Sparse Core Ops, SparseCore 0:
  33.4 134.8 all-reduce.6
  326.1 212.3 all-gather.2
  737.5 135.4 all-reduce.4
